TPU v7x, 512 devices: a whole 4x8x8 slice. The times are simulated.
512 devices in a mesh: wide: 128 (over y, z, core), rep: 4 (over x).
Axes of the slice: x: 4, y: 8, z: 8, core: 2. Of those that a mesh axis runs over, the one named last changes fastest.
Arguments:
- node_feats: bfloat16 [131072, 512], P('wide'), may hold values from -6 to 6
- w_self: bfloat16 [512, 512], replicated, may hold values from -0.25 to 0.25
- w_neigh: bfloat16 [512, 512], replicated, may hold values from -0.25 to 0.25
- send_rows: int32 [128, 128, 32], P('wide', None, 'rep'), may hold values from 0 to 1023
- tile_dst: int32 [128, 4, 128], P('wide', 'rep'), may hold values from 0 to 15
- tile_src: int32 [128, 4, 128], P('wide', 'rep'), may hold values from 0 to 31
- tile_bits: int32 [128, 4, 32768], P('wide', 'rep'), may hold values from 0 to 65280
- norm_count: int32 [131072], P('wide'), may hold values from 512 to 2048
- grad_out: bfloat16 [131072, 512], P(('wide', 'rep')), may hold values from -6 to 6
Outputs:
- out_feats: bfloat16 [131072, 512], P(('wide', 'rep'))
- grad_feats: bfloat16 [131072, 512], P(('wide', 'rep'))
- grad_self: bfloat16 [512, 512], replicated
- grad_neigh: bfloat16 [512, 512], replicated
All inputs are finite; a program needn't handle non-finite values.
Results may differ from a plain program's by a relative error of at most 0.014.
Values may be sent and summed in bfloat16 or wider, within the bound.
No kernel may reach another device: no remote copies, remote signals or barrier semaphores. Data moves between devices by JAX's collectives and lax.ppermute only.
A program may use at most 64 MiB of HBM per device.

v0:
```python
import math
import jax
import jax.numpy as jnp
from jax import lax
from jax.sharding import PartitionSpec as P

BLOCK = 64


def unpack_bits(packed, tile_count, block_size):
    shaped = packed.reshape(tile_count, block_size, block_size // 16)
    shift_list = jnp.arange(16, dtype=jnp.int32)
    bit_grid = jnp.bitwise_and(jnp.right_shift(shaped[..., None], shift_list), 1)
    return bit_grid.reshape(tile_count, block_size, block_size)


def times_transposed(left, right):
    return lax.dot_general(
        left, right, (((1,), (1,)), ((), ())), preferred_element_type=jnp.float32
    )


def on_device(
    node_feats, w_self, w_neigh, send_rows, tile_dst, tile_src, tile_bits, norm_count, grad_out
):
    node_rows, feat_width = node_feats.shape
    peer_count = lax.axis_size("wide")
    replicas = lax.axis_size("rep")
    slot_count = send_rows.shape[2]
    tile_total = tile_dst.shape[2]
    block_size = BLOCK
    quarter = node_rows // replicas
    rep_index = lax.axis_index("rep")
    dst_count = node_rows // block_size
    group_size = math.gcd(tile_total, 32)
    send_index = send_rows[0]
    outgoing = jnp.take(node_feats, send_index.reshape(-1), axis=0).reshape(
        peer_count, slot_count, feat_width
    )
    incoming = lax.all_to_all(outgoing, "wide", split_axis=0, concat_axis=0, tiled=True)
    src_table = jnp.concatenate(
        [node_feats, incoming.reshape(peer_count * slot_count, feat_width)], axis=0
    )
    source_blocks = src_table.reshape(-1, block_size, feat_width)
    src_count = source_blocks.shape[0]
    tile_masks = unpack_bits(tile_bits[0, 0], tile_total, block_size).astype(jnp.bfloat16)
    grouped_masks = tile_masks.reshape(-1, group_size, block_size, block_size)
    grouped_dst = tile_dst[0, 0].reshape(-1, group_size)
    grouped_src = tile_src[0, 0].reshape(-1, group_size)

    def forward_group(running, group_items):
        mask_part, dst_part, src_part = group_items
        picked = jnp.take(source_blocks, src_part, axis=0)
        products = jnp.einsum("tij,tjf->tif", mask_part, picked, preferred_element_type=jnp.float32)
        return (running.at[dst_part].add(products), None)

    partial_sum, _ = lax.scan(
        forward_group,
        jnp.zeros((dst_count, block_size, feat_width), jnp.float32),
        (grouped_masks, grouped_dst, grouped_src),
    )
    partial_sum = partial_sum.reshape(node_rows, feat_width)
    summed = lax.psum(partial_sum, "rep")
    own_sums = lax.dynamic_slice_in_dim(summed, rep_index * quarter, quarter, 0)
    scale_all = lax.rsqrt(norm_count.astype(jnp.float32))
    own_scale = lax.dynamic_slice_in_dim(scale_all, rep_index * quarter, quarter, 0)
    own_feats = lax.dynamic_slice_in_dim(node_feats, rep_index * quarter, quarter, 0)
    own_agg = (own_sums * own_scale[:, None]).astype(jnp.bfloat16)
    pre_act = jnp.dot(own_feats, w_self, preferred_element_type=jnp.float32) + jnp.dot(
        own_agg, w_neigh, preferred_element_type=jnp.float32
    )
    sigmoid = jax.nn.sigmoid(pre_act)
    out_feats = (pre_act * sigmoid).astype(jnp.bfloat16)
    grad_pre = (grad_out.astype(jnp.float32) * sigmoid * (1.0 + pre_act * (1.0 - sigmoid))).astype(
        jnp.bfloat16
    )
    dims_rows = (((0,), (0,)), ((), ()))
    self_term = lax.dot_general(own_feats, grad_pre, dims_rows, preferred_element_type=jnp.float32)
    neigh_term = lax.dot_general(own_agg, grad_pre, dims_rows, preferred_element_type=jnp.float32)
    summed_self, summed_neigh = lax.psum((self_term, neigh_term), ("wide", "rep"))
    own_grad_agg = (times_transposed(grad_pre, w_neigh) * own_scale[:, None]).astype(jnp.bfloat16)
    grad_agg = lax.all_gather(own_grad_agg, "rep", axis=0, tiled=True)
    agg_blocks = grad_agg.reshape(dst_count, block_size, feat_width)

    def backward_group(running, group_items):
        mask_part, dst_part, src_part = group_items
        picked = jnp.take(agg_blocks, dst_part, axis=0)
        products = jnp.einsum("tij,tif->tjf", mask_part, picked, preferred_element_type=jnp.float32)
        return (running.at[src_part].add(products), None)

    table_grad, _ = lax.scan(
        backward_group,
        jnp.zeros((src_count, block_size, feat_width), jnp.float32),
        (grouped_masks, grouped_dst, grouped_src),
    )
    table_grad = table_grad.reshape(src_count * block_size, feat_width)
    local_grad = table_grad[:node_rows]
    halo_grad = (
        table_grad[node_rows:].astype(jnp.bfloat16).reshape(peer_count, slot_count, feat_width)
    )
    returned = lax.all_to_all(halo_grad, "wide", split_axis=0, concat_axis=0, tiled=True)
    returned_rows = (
        jnp.zeros((node_rows, feat_width), jnp.float32)
        .at[send_index.reshape(-1)]
        .add(returned.reshape(-1, feat_width).astype(jnp.float32))
    )
    own_total = lax.psum_scatter(
        (local_grad + returned_rows).astype(jnp.bfloat16), "rep", scatter_dimension=0, tiled=True
    ).astype(jnp.float32)
    grad_feats = (own_total + times_transposed(grad_pre, w_self)).astype(jnp.bfloat16)
    return (
        out_feats,
        grad_feats,
        summed_self.astype(jnp.bfloat16),
        summed_neigh.astype(jnp.bfloat16),
    )


def solution(mesh):
    in_specs = (
        P("wide", None),
        P(),
        P(),
        P("wide", None, "rep"),
        P("wide", "rep", None),
        P("wide", "rep", None),
        P("wide", "rep", None),
        P("wide"),
        P(("wide", "rep"), None),
    )
    out_specs = (P(("wide", "rep"), None), P(("wide", "rep"), None), P(), P())
    return jax.shard_map(
        on_device, mesh=mesh, in_specs=in_specs, out_specs=out_specs, check_vma=False
    )
```

profile of v0, /device:TPU:1, one launch (start us, length us, event | category | flops | bytes accessed | tf_op | source)
XLA Modules:
  0.0 459.9 jit_solution(16109861953868291241)
XLA Ops:
  9.0 5.4 %gather_fusion.2 = bf16[1024,512]{1,0:T(8,128)(2,1)S(1)} fusion(bf16[1024,512]{1,0:T(8,128)(2,1)} %param.13, s32[1024]{0:T(1024)S(1)} %broadcast_clamp_fusion), kind=kCustom, calls=%fused_computation.2 | custom fusion | bytes 2101248 | tf_op jit(solution)/shard_map/jit(_take)/gather | solution.py:37
  15.5 18.4 %all-to-all-start = ((bf16[128,8,512]{2,1,0:T(8,128)(2,1)}), bf16[128,8,512]{2,1,0:T(8,128)(2,1)S(1)}, u32[]{:S(2)}, u32[]{:S(2)}) async-start(bf16[128,8,512]{2,1,0:T(8,128)(2,1)} %bitcast_select_fusion), calls=%async_computation | async-start | bytes 2097152 | tf_op jit(solution)/shard_map/all_to_all | solution.py:40
  37.1 5.7 %shift_right_arithmetic.23 = s32[128,64,4]{2,1,0:T(8,128)} reshape(s32[32768]{0:T(1024)S(1)} %reduce.10) | data formatting | bytes 262144 | tf_op jit(solution)/shard_map/shift_right_arithmetic | solution.py:13
  48.2 16.2 %all-to-all-done = bf16[128,8,512]{2,1,0:T(8,128)(2,1)S(1)} async-done(((bf16[128,8,512]{2,1,0:T(8,128)(2,1)}), bf16[128,8,512]{2,1,0:T(8,128)(2,1)S(1)}, u32[]{:S(2)}, u32[]{:S(2)}) %all-to-all-start) | async-done | bytes 1048608 | tf_op jit(solution)/shard_map/all_to_all | solution.py:40
  66.1 58.5 %while.20 = (s32[]{:T(128)}, f32[16,64,512]{2,1,0:T(8,128)S(1)}, s32[4,32]{1,0:T(4,128)S(1)}, bf16[4,32,64,64]{2,3,1,0:T(8,128)(2,1)}, s32[4,32]{1,0:T(4,128)S(1)}, /*index=5*/bf16[32,64,512]{2,1,0:T(8,128)(2,1)}, s32[]{:T(128)}) while((s32[]{:T(128)}, f32[16,64,512]{2,1,0:T(8,128)S(1)}, s32[4,32]{1,0:T(4,128)S(1)}, ...), condition=%wide.region_2.3_spmd, body=%wide.region_0.0_spmd.sunk | while | flops 136316288 | bytes 23598240 | solution.py:57
  66.2 3.6 gather_fusion
  69.8 4.5 fusion.53
  74.3 6.5 %scatter_fusion = f32[16,64,512]{2,1,0:T(8,128)S(1)} fusion(f32[16,64,512]{2,1,0:T(8,128)S(1)} %get-tuple-element.204, s32[32]{0:T(128)S(1)} %get-tuple-element.186, f32[32,64,512]{2,1,0:T(8,128)} %fusion.53), kind=kCustom, calls=%fused_computation.3.clone.1 | custom fusion | flops 1048576 | bytes 12583040 | tf_op jit(solution)/shard_map/while/body/eval_jaxpr/scatter-add | solution.py:55
  80.8 3.6 gather_fusion
  84.4 4.5 fusion.53
  88.9 6.5 %scatter_fusion = f32[16,64,512]{2,1,0:T(8,128)S(1)} fusion(f32[16,64,512]{2,1,0:T(8,128)S(1)} %get-tuple-element.204, s32[32]{0:T(128)S(1)} %get-tuple-element.186, f32[32,64,512]{2,1,0:T(8,128)} %fusion.53), kind=kCustom, calls=%fused_computation.3.clone.1 | custom fusion | flops 1048576 | bytes 12583040 | tf_op jit(solution)/shard_map/while/body/eval_jaxpr/scatter-add | solution.py:55
  95.4 3.6 gather_fusion
  99.1 4.5 fusion.53
  103.5 6.5 %scatter_fusion = f32[16,64,512]{2,1,0:T(8,128)S(1)} fusion(f32[16,64,512]{2,1,0:T(8,128)S(1)} %get-tuple-element.204, s32[32]{0:T(128)S(1)} %get-tuple-element.186, f32[32,64,512]{2,1,0:T(8,128)} %fusion.53), kind=kCustom, calls=%fused_computation.3.clone.1 | custom fusion | flops 1048576 | bytes 12583040 | tf_op jit(solution)/shard_map/while/body/eval_jaxpr/scatter-add | solution.py:55
  110.1 3.6 gather_fusion
  113.7 4.5 fusion.53
  118.2 6.5 %scatter_fusion = f32[16,64,512]{2,1,0:T(8,128)S(1)} fusion(f32[16,64,512]{2,1,0:T(8,128)S(1)} %get-tuple-element.204, s32[32]{0:T(128)S(1)} %get-tuple-element.186, f32[32,64,512]{2,1,0:T(8,128)} %fusion.53), kind=kCustom, calls=%fused_computation.3.clone.1 | custom fusion | flops 1048576 | bytes 12583040 | tf_op jit(solution)/shard_map/while/body/eval_jaxpr/scatter-add | solution.py:55
  127.6 62.0 %all-reduce.4.cloned.1.call-done = f32[1024,512]{1,0:T(8,128)} async-done(((f32[1024,512]{1,0:T(8,128)}), f32[1024,512]{1,0:T(8,128)}) %all-reduce.4.cloned.1.call-update) | async-done | bytes 2097168 | tf_op jit(solution)/shard_map/psum | solution.py:63
  193.0 28.4 %all-gather.2.cloned.1.call-done = bf16[1024,512]{1,0:T(8,128)(2,1)} async-done(((bf16[256,512]{1,0:T(8,128)(2,1)}), bf16[1024,512]{1,0:T(8,128)(2,1)}) %all-gather.2.cloned.1.call-update) | async-done | bytes 1048592 | tf_op jit(solution)/shard_map/all_gather | solution.py:82
  223.9 62.5 %while.21 = (s32[]{:T(128)}, f32[32,64,512]{2,1,0:T(8,128)}, s32[4,32]{1,0:T(4,128)S(1)}, bf16[4,32,64,64]{2,3,1,0:T(8,128)(2,1)}, s32[4,32]{1,0:T(4,128)S(1)}, /*index=5*/bf16[16,64,512]{2,1,0:T(8,128)(2,1)}, s32[]{:T(128)}) while((s32[]{:T(128)}, f32[32,64,512]{2,1,0:T(8,128)}, s32[4,32]{1,0:T(4,128)S(1)}, ...), condition=%wide.region_6.7_spmd, body=%wide.region_4.6_spmd.sunk | while | flops 136316288 | bytes 23598240 | solution.py:91
  225.9 3.8 fusion.57
  229.7 9.8 %scatter_fusion.1 = f32[32,64,512]{2,1,0:T(8,128)} fusion(f32[32,64,512]{2,1,0:T(8,128)} %get-tuple-element.225, s32[32]{0:T(128)S(1)} %get-tuple-element.194, f32[32,64,512]{2,1,0:T(8,128)} %fusion.57), kind=kCustom, calls=%fused_computation.4.clone.1 | custom fusion | flops 1048576 | bytes 12583040 | tf_op jit(solution)/shard_map/while/body/eval_jaxpr/scatter-add | solution.py:89
  241.4 3.7 fusion.57
  245.1 9.8 %scatter_fusion.1 = f32[32,64,512]{2,1,0:T(8,128)} fusion(f32[32,64,512]{2,1,0:T(8,128)} %get-tuple-element.225, s32[32]{0:T(128)S(1)} %get-tuple-element.194, f32[32,64,512]{2,1,0:T(8,128)} %fusion.57), kind=kCustom, calls=%fused_computation.4.clone.1 | custom fusion | flops 1048576 | bytes 12583040 | tf_op jit(solution)/shard_map/while/body/eval_jaxpr/scatter-add | solution.py:89
  256.9 3.7 fusion.57
  260.6 10.0 %scatter_fusion.1 = f32[32,64,512]{2,1,0:T(8,128)} fusion(f32[32,64,512]{2,1,0:T(8,128)} %get-tuple-element.225, s32[32]{0:T(128)S(1)} %get-tuple-element.194, f32[32,64,512]{2,1,0:T(8,128)} %fusion.57), kind=kCustom, calls=%fused_computation.4.clone.1 | custom fusion | flops 1048576 | bytes 12583040 | tf_op jit(solution)/shard_map/while/body/eval_jaxpr/scatter-add | solution.py:89
  272.6 3.7 fusion.57
  276.3 10.1 %scatter_fusion.1 = f32[32,64,512]{2,1,0:T(8,128)} fusion(f32[32,64,512]{2,1,0:T(8,128)} %get-tuple-element.225, s32[32]{0:T(128)S(1)} %get-tuple-element.194, f32[32,64,512]{2,1,0:T(8,128)} %fusion.57), kind=kCustom, calls=%fused_computation.4.clone.1 | custom fusion | flops 1048576 | bytes 12583040 | tf_op jit(solution)/shard_map/while/body/eval_jaxpr/scatter-add | solution.py:89
  289.2 15.9 %all-to-all-start.1 = ((bf16[128,8,512]{2,1,0:T(8,128)(2,1)}), bf16[128,8,512]{2,1,0:T(8,128)(2,1)}, u32[]{:S(2)}, u32[]{:S(2)}) async-start(bf16[128,8,512]{2,1,0:T(8,128)(2,1)} %bitcast.21), calls=%async_computation.1 | async-start | bytes 2097152 | tf_op jit(solution)/shard_map/all_to_all | solution.py:101
  307.0 28.2 %all-to-all-done.1 = bf16[128,8,512]{2,1,0:T(8,128)(2,1)} async-done(((bf16[128,8,512]{2,1,0:T(8,128)(2,1)}), bf16[128,8,512]{2,1,0:T(8,128)(2,1)}, u32[]{:S(2)}, u32[]{:S(2)}) %all-to-all-start.1) | async-done | bytes 1048608 | tf_op jit(solution)/shard_map/all_to_all | solution.py:101
  335.2 8.0 %scatter_custom_fusion.2 = f32[1024,512]{1,0:T(8,128)S(1)} fusion(f32[1024,512]{1,0:T(8,128)S(1)} %bitcast.83, s32[1024]{0:T(1024)S(1)} %bitcast.86, bf16[128,8,512]{2,1,0:T(8,128)(2,1)} %all-to-all-done.1), kind=kCustom, calls=%fused_computation.45 | custom fusion | flops 1048576 | bytes 3145728 | tf_op jit(solution)/shard_map/scatter-add | solution.py:105
  347.0 104.4 %all-reduce.5 = (bf16[512,512]{1,0:T(8,128)(2,1)}, bf16[512,512]{1,0:T(8,128)(2,1)}) all-reduce(f32[512,512]{1,0:T(8,128)S(1)} %fusion.27, f32[512,512]{1,0:T(8,128)S(1)} %fusion.33), channel_id=1, replica_groups=mesh['wide'=128,'rep'=4] {'wide','rep'}, use_global_device_ids=true, to_apply=%region_9.10 | all-reduce | flops 524288 | bytes 3145728 | tf_op jit(solution)/shard_map/psum | solution.py:80
  (83 shorter events, 40.4 us)
Async XLA Ops:
  7.2 182.5 %copy-start = (bf16[512,512]{1,0:T(8,128)(2,1)S(1)}, bf16[512,512]{1,0:T(8,128)(2,1)}, u32[]{:S(2)}) copy-start(bf16[512,512]{1,0:T(8,128)(2,1)} %param.15) | copy-start | bytes 1572868
  14.3 20.2 %copy-start.6 = (s32[1,1,128]{2,1,0:T(1,128)S(1)}, s32[1,1,128]{2,1,0:T(1,128)}, u32[]{:S(2)}) copy-start(s32[1,1,128]{2,1,0:T(1,128)} %param.17) | copy-start | bytes 1540
  14.3 20.9 %copy-start.7 = (s32[1,1,128]{2,1,0:T(1,128)S(1)}, s32[1,1,128]{2,1,0:T(1,128)}, u32[]{:S(2)}) copy-start(s32[1,1,128]{2,1,0:T(1,128)} %param.18) | copy-start | bytes 1540
  14.4 21.8 %copy-start.4 = (s32[1,1,32768]{2,1,0:T(1,128)S(1)}, s32[1,1,32768]{2,1,0:T(1,128)}, u32[]{:S(2)}) copy-start(s32[1,1,32768]{2,1,0:T(1,128)} %param.19) | copy-start | bytes 393220
  15.5 48.9 %all-to-all-start = ((bf16[128,8,512]{2,1,0:T(8,128)(2,1)}), bf16[128,8,512]{2,1,0:T(8,128)(2,1)S(1)}, u32[]{:S(2)}, u32[]{:S(2)}) async-start(bf16[128,8,512]{2,1,0:T(8,128)(2,1)} %bitcast_select_fusion), calls=%async_computation | async-start | bytes 2097152 | tf_op jit(solution)/shard_map/all_to_all | solution.py:40
  34.0 155.7 %all-reduce.4.cloned.1.call-start = ((), (), s32[]{:S(2)}) async-start(), calls=%async_computation.3 | async-start | bytes 4194304 | tf_op jit(solution)/shard_map/psum | solution.py:63
  46.1 18.3 %copy-start.2 = (bf16[1024,512]{1,0:T(8,128)(2,1)S(1)}, bf16[1024,512]{1,0:T(8,128)(2,1)}, u32[]{:S(2)}) copy-start(bf16[1024,512]{1,0:T(8,128)(2,1)} %param.13) | copy-start | bytes 3145732
  124.7 1.3 copy-start.1
  124.7 1.6 copy-start.5
  124.7 1.7 copy-start.3
  126.0 95.4 %all-gather.2.cloned.1.call-start = ((), (), s32[]{:S(2)}) async-start(), calls=%async_computation.4 | async-start | bytes 1310720 | tf_op jit(solution)/shard_map/all_gather | solution.py:82
  289.2 46.0 %all-to-all-start.1 = ((bf16[128,8,512]{2,1,0:T(8,128)(2,1)}), bf16[128,8,512]{2,1,0:T(8,128)(2,1)}, u32[]{:S(2)}, u32[]{:S(2)}) async-start(bf16[128,8,512]{2,1,0:T(8,128)(2,1)} %bitcast.21), calls=%async_computation.1 | async-start | bytes 2097152 | tf_op jit(solution)/shard_map/all_to_all | solution.py:101
  305.1 146.3 %reduce-scatter.2.cloned.1.call-start = ((), (), s32[]{:S(2)}) async-start(), calls=%async_computation.5 | async-start | bytes 1310720 | tf_op jit(solution)/shard_map/reduce_scatter | solution.py:107
Sparse Core Ops, SparseCore 0:
  126.2 63.4 all-reduce.3
  193.2 28.2 all-gather.1
  344.4 20.2 reduce-scatter.1
where the time goes:
time: 462 us; the launch traced here: 460 us
  waiting for transfers between devices  135 us (29%)
  blocking collectives  104 us (23%)
  other arithmetic  82.7 us (18%)
  local copies, waits for them, and re-layouts  47 us (10%)
  matrix products  42.2 us (9%)
  starting transfers between devices  34.6 us (7%)
  between operations  14 us (3%)
    psum x1, blocking collectives, on_device(): lax.psum((self_term, neigh_term), ('wide', 'rep'))  104 us
    psum x1, waiting for transfers between devices, on_device(): summed = lax.psum(partial_sum, 'rep')  62 us
    scatter-add x4, other arithmetic, backward_group(): return (running.at[src_part].add(products), None)  39.6 us
    all_gather x1, waiting for transfers between devices, on_device(): grad_agg = lax.all_gather(own_grad_agg, 'rep', axis=0, tiled=True)  28.4 us
    all_to_all x1, waiting for transfers between devices, on_device(): lax.all_to_all(halo_grad, 'wide', split_axis=0, concat_axis=0, tiled=True)  28.2 us
    scatter-add x4, other arithmetic, forward_group(): return (running.at[dst_part].add(products), None)  25.9 us
    all_to_all x1, starting transfers between devices, on_device(): lax.all_to_all(outgoing, 'wide', split_axis=0, concat_axis=0, tiled=True)  18.4 us
    dot_general x4, matrix products, forward_group(): jnp.einsum('tij,tjf->tif', mask_part, picked, preferred_element_type=jnp....  17.9 us
  transfers between devices with their start and end apart: 5, of which 4 were waited for; matrix products, arithmetic and copies ran while one was open for 4% of the time, Pallas kernels for 0%

commit v1 on v0

--- a/solution.py
+++ b/solution.py
@@ -77,7 +77,7 @@
     dims_rows = (((0,), (0,)), ((), ()))
     self_term = lax.dot_general(own_feats, grad_pre, dims_rows, preferred_element_type=jnp.float32)
     neigh_term = lax.dot_general(own_agg, grad_pre, dims_rows, preferred_element_type=jnp.float32)
-    summed_self, summed_neigh = lax.psum((self_term, neigh_term), ("wide", "rep"))
+    summed_self, summed_neigh = lax.psum(lax.psum((self_term, neigh_term), "wide"), "rep")
     own_grad_agg = (times_transposed(grad_pre, w_neigh) * own_scale[:, None]).astype(jnp.bfloat16)
     grad_agg = lax.all_gather(own_grad_agg, "rep", axis=0, tiled=True)
     agg_blocks = grad_agg.reshape(dst_count, block_size, feat_width)

time: 462 us -> 575 us (1.24)
  waiting for transfers between devices: 135 us -> 298 us
  blocking collectives: 104 us -> 46.9 us
    psum x0 -> x1, waiting for transfers between devices: none -> 168 us  [on_device(): lax.psum((self_term, neigh_term), 'wide')]
    psum x1, blocking collectives: 104 us -> 46.9 us  [on_device(): lax.psum(lax.psum((self_term, neigh_term), 'wide'), 'rep')]
  transfers between devices with their start and end apart: 5 -> 6, of which waited for: 4 -> 5; matrix products, arithmetic and copies ran while one was open for 4% -> 5% of each run, Pallas kernels for 0% -> 0%
where the time goes in v1:
time: 575 us; the launch traced here: 568 us
  waiting for transfers between devices  298 us (52%)
  other arithmetic  82.7 us (14%)
  local copies, waits for them, and re-layouts  47 us (8%)
  blocking collectives  46.9 us (8%)
  matrix products  44.2 us (8%)
  starting transfers between devices  34.6 us (6%)
  between operations  14 us (2%)
    psum x1, waiting for transfers between devices, on_device(): lax.psum((self_term, neigh_term), 'wide')  168 us
    psum x1, waiting for transfers between devices, on_device(): summed = lax.psum(partial_sum, 'rep')  62 us
    psum x1, blocking collectives, on_device(): lax.psum(lax.psum((self_term, neigh_term), 'wide'), 'rep')  46.9 us
    scatter-add x4, other arithmetic, backward_group(): return (running.at[src_part].add(products), None)  39.6 us
    all_gather x1, waiting for transfers between devices, on_device(): grad_agg = lax.all_gather(own_grad_agg, 'rep', axis=0, tiled=True)  28.4 us
    scatter-add x4, other arithmetic, forward_group(): return (running.at[dst_part].add(products), None)  25.9 us
    all_to_all x1, waiting for transfers between devices, on_device(): lax.all_to_all(halo_grad, 'wide', split_axis=0, concat_axis=0, tiled=True)  23.6 us
    all_to_all x1, starting transfers between devices, on_device(): lax.all_to_all(outgoing, 'wide', split_axis=0, concat_axis=0, tiled=True)  18.4 us
  transfers between devices with their start and end apart: 6, of which 5 were waited for; matrix products, arithmetic and copies ran while one was open for 5% of the time, Pallas kernels for 0%

profile of v1, /device:TPU:1, one launch (start us, length us, event | category | flops | bytes accessed | tf_op | source)
XLA Modules:
  0.0 567.5 jit_solution(10825546299449742621)
XLA Ops:
  9.0 5.4 gather_fusion.2
  15.6 18.4 %all-to-all-start = ((bf16[128,8,512]{2,1,0:T(8,128)(2,1)}), bf16[128,8,512]{2,1,0:T(8,128)(2,1)S(1)}, u32[]{:S(2)}, u32[]{:S(2)}) async-start(bf16[128,8,512]{2,1,0:T(8,128)(2,1)} %bitcast_select_fusion), calls=%async_computation | async-start | bytes 2097152 | tf_op jit(solution)/shard_map/all_to_all | solution.py:40
  37.1 5.7 shift_right_arithmetic.23
  48.3 16.2 %all-to-all-done = bf16[128,8,512]{2,1,0:T(8,128)(2,1)S(1)} async-done(((bf16[128,8,512]{2,1,0:T(8,128)(2,1)}), bf16[128,8,512]{2,1,0:T(8,128)(2,1)S(1)}, u32[]{:S(2)}, u32[]{:S(2)}) %all-to-all-start) | async-done | bytes 1048608 | tf_op jit(solution)/shard_map/all_to_all | solution.py:40
  66.1 58.6 %while.20 = (s32[]{:T(128)}, f32[16,64,512]{2,1,0:T(8,128)S(1)}, s32[4,32]{1,0:T(4,128)S(1)}, bf16[4,32,64,64]{2,3,1,0:T(8,128)(2,1)}, s32[4,32]{1,0:T(4,128)S(1)}, /*index=5*/bf16[32,64,512]{2,1,0:T(8,128)(2,1)}, s32[]{:T(128)}) while((s32[]{:T(128)}, f32[16,64,512]{2,1,0:T(8,128)S(1)}, s32[4,32]{1,0:T(4,128)S(1)}, ...), condition=%wide.region_2.3_spmd, body=%wide.region_0.0_spmd.sunk | while | flops 136316288 | bytes 23598240 | solution.py:57
  66.2 3.6 gather_fusion
  69.8 4.5 fusion.53
  74.3 6.5 %scatter_fusion = f32[16,64,512]{2,1,0:T(8,128)S(1)} fusion(f32[16,64,512]{2,1,0:T(8,128)S(1)} %get-tuple-element.206, s32[32]{0:T(128)S(1)} %get-tuple-element.188, f32[32,64,512]{2,1,0:T(8,128)} %fusion.53), kind=kCustom, calls=%fused_computation.3.clone.1 | custom fusion | flops 1048576 | bytes 12583040 | tf_op jit(solution)/shard_map/while/body/eval_jaxpr/scatter-add | solution.py:55
  80.8 3.6 gather_fusion
  84.4 4.5 fusion.53
  88.9 6.5 %scatter_fusion = f32[16,64,512]{2,1,0:T(8,128)S(1)} fusion(f32[16,64,512]{2,1,0:T(8,128)S(1)} %get-tuple-element.206, s32[32]{0:T(128)S(1)} %get-tuple-element.188, f32[32,64,512]{2,1,0:T(8,128)} %fusion.53), kind=kCustom, calls=%fused_computation.3.clone.1 | custom fusion | flops 1048576 | bytes 12583040 | tf_op jit(solution)/shard_map/while/body/eval_jaxpr/scatter-add | solution.py:55
  95.5 3.6 gather_fusion
  99.1 4.5 fusion.53
  103.5 6.5 %scatter_fusion = f32[16,64,512]{2,1,0:T(8,128)S(1)} fusion(f32[16,64,512]{2,1,0:T(8,128)S(1)} %get-tuple-element.206, s32[32]{0:T(128)S(1)} %get-tuple-element.188, f32[32,64,512]{2,1,0:T(8,128)} %fusion.53), kind=kCustom, calls=%fused_computation.3.clone.1 | custom fusion | flops 1048576 | bytes 12583040 | tf_op jit(solution)/shard_map/while/body/eval_jaxpr/scatter-add | solution.py:55
  113.7 4.5 fusion.53
  118.2 6.5 %scatter_fusion = f32[16,64,512]{2,1,0:T(8,128)S(1)} fusion(f32[16,64,512]{2,1,0:T(8,128)S(1)} %get-tuple-element.206, s32[32]{0:T(128)S(1)} %get-tuple-element.188, f32[32,64,512]{2,1,0:T(8,128)} %fusion.53), kind=kCustom, calls=%fused_computation.3.clone.1 | custom fusion | flops 1048576 | bytes 12583040 | tf_op jit(solution)/shard_map/while/body/eval_jaxpr/scatter-add | solution.py:55
  127.6 62.0 %all-reduce.6.cloned.1.call-done = f32[1024,512]{1,0:T(8,128)} async-done(((f32[1024,512]{1,0:T(8,128)}), f32[1024,512]{1,0:T(8,128)}) %all-reduce.6.cloned.1.call-update) | async-done | bytes 2097168 | tf_op jit(solution)/shard_map/psum | solution.py:63
  193.1 28.4 %all-gather.2.cloned.1.call-done = bf16[1024,512]{1,0:T(8,128)(2,1)} async-done(((bf16[256,512]{1,0:T(8,128)(2,1)}), bf16[1024,512]{1,0:T(8,128)(2,1)}) %all-gather.2.cloned.1.call-update) | async-done | bytes 1048592 | tf_op jit(solution)/shard_map/all_gather | solution.py:82
  224.0 62.4 %while.21 = (s32[]{:T(128)}, f32[32,64,512]{2,1,0:T(8,128)}, s32[4,32]{1,0:T(4,128)S(1)}, bf16[4,32,64,64]{2,3,1,0:T(8,128)(2,1)}, s32[4,32]{1,0:T(4,128)S(1)}, /*index=5*/bf16[16,64,512]{2,1,0:T(8,128)(2,1)}, s32[]{:T(128)}) while((s32[]{:T(128)}, f32[32,64,512]{2,1,0:T(8,128)}, s32[4,32]{1,0:T(4,128)S(1)}, ...), condition=%wide.region_6.7_spmd, body=%wide.region_4.6_spmd.sunk | while | flops 136316288 | bytes 23598240 | solution.py:91
  225.9 3.8 fusion.57
  229.7 9.7 %scatter_fusion.1 = f32[32,64,512]{2,1,0:T(8,128)} fusion(f32[32,64,512]{2,1,0:T(8,128)} %get-tuple-element.227, s32[32]{0:T(128)S(1)} %get-tuple-element.196, f32[32,64,512]{2,1,0:T(8,128)} %fusion.57), kind=kCustom, calls=%fused_computation.4.clone.1 | custom fusion | flops 1048576 | bytes 12583040 | tf_op jit(solution)/shard_map/while/body/eval_jaxpr/scatter-add | solution.py:89
  241.4 3.7 fusion.57
  245.1 9.9 %scatter_fusion.1 = f32[32,64,512]{2,1,0:T(8,128)} fusion(f32[32,64,512]{2,1,0:T(8,128)} %get-tuple-element.227, s32[32]{0:T(128)S(1)} %get-tuple-element.196, f32[32,64,512]{2,1,0:T(8,128)} %fusion.57), kind=kCustom, calls=%fused_computation.4.clone.1 | custom fusion | flops 1048576 | bytes 12583040 | tf_op jit(solution)/shard_map/while/body/eval_jaxpr/scatter-add | solution.py:89
  256.9 3.8 fusion.57
  260.7 9.9 %scatter_fusion.1 = f32[32,64,512]{2,1,0:T(8,128)} fusion(f32[32,64,512]{2,1,0:T(8,128)} %get-tuple-element.227, s32[32]{0:T(128)S(1)} %get-tuple-element.196, f32[32,64,512]{2,1,0:T(8,128)} %fusion.57), kind=kCustom, calls=%fused_computation.4.clone.1 | custom fusion | flops 1048576 | bytes 12583040 | tf_op jit(solution)/shard_map/while/body/eval_jaxpr/scatter-add | solution.py:89
  272.6 3.7 fusion.57
  276.3 10.0 %scatter_fusion.1 = f32[32,64,512]{2,1,0:T(8,128)} fusion(f32[32,64,512]{2,1,0:T(8,128)} %get-tuple-element.227, s32[32]{0:T(128)S(1)} %get-tuple-element.196, f32[32,64,512]{2,1,0:T(8,128)} %fusion.57), kind=kCustom, calls=%fused_computation.4.clone.1 | custom fusion | flops 1048576 | bytes 12583040 | tf_op jit(solution)/shard_map/while/body/eval_jaxpr/scatter-add | solution.py:89
  289.1 15.9 %all-to-all-start.1 = ((bf16[128,8,512]{2,1,0:T(8,128)(2,1)}), bf16[128,8,512]{2,1,0:T(8,128)(2,1)}, u32[]{:S(2)}, u32[]{:S(2)}) async-start(bf16[128,8,512]{2,1,0:T(8,128)(2,1)} %bitcast.21), calls=%async_computation.1 | async-start | bytes 2097152 | tf_op jit(solution)/shard_map/all_to_all | solution.py:101
  311.7 23.6 %all-to-all-done.1 = bf16[128,8,512]{2,1,0:T(8,128)(2,1)} async-done(((bf16[128,8,512]{2,1,0:T(8,128)(2,1)}), bf16[128,8,512]{2,1,0:T(8,128)(2,1)}, u32[]{:S(2)}, u32[]{:S(2)}) %all-to-all-start.1) | async-done | bytes 1048608 | tf_op jit(solution)/shard_map/all_to_all | solution.py:101
  335.3 8.0 %scatter_custom_fusion.2 = f32[1024,512]{1,0:T(8,128)S(1)} fusion(f32[1024,512]{1,0:T(8,128)S(1)} %bitcast.83, s32[1024]{0:T(1024)S(1)} %bitcast.86, bf16[128,8,512]{2,1,0:T(8,128)(2,1)} %all-to-all-done.1), kind=kCustom, calls=%fused_computation.45 | custom fusion | flops 1048576 | bytes 3145728 | tf_op jit(solution)/shard_map/scatter-add | solution.py:105
  344.4 167.7 %all-reduce.8.cloned.1.call-done = (f32[512,512]{1,0:T(8,128)}, f32[512,512]{1,0:T(8,128)}) async-done(((f32[512,512]{1,0:T(8,128)}, f32[512,512]{1,0:T(8,128)}), (f32[512,512]{1,0:T(8,128)}, f32[512,512]{1,0:T(8,128)})) %all-reduce.8.cloned.1.call-update) | async-done | bytes 2097168 | tf_op jit(solution)/shard_map/psum | solution.py:80
  512.1 46.9 %all-reduce.9 = (bf16[512,512]{1,0:T(8,128)(2,1)}, bf16[512,512]{1,0:T(8,128)(2,1)}) all-reduce(f32[512,512]{1,0:T(8,128)} %get-tuple-element.106, f32[512,512]{1,0:T(8,128)} %get-tuple-element.107), channel_id=1, replica_groups=mesh['wide'=128,'rep'=4] {'rep'}, use_global_device_ids=true, to_apply=%region_10.11 | all-reduce | flops 524288 | bytes 3145728 | tf_op jit(solution)/shard_map/psum | solution.py:80
  (86 shorter events, 46.1 us)
Async XLA Ops:
  7.2 182.5 %copy-start = (bf16[512,512]{1,0:T(8,128)(2,1)S(1)}, bf16[512,512]{1,0:T(8,128)(2,1)}, u32[]{:S(2)}) copy-start(bf16[512,512]{1,0:T(8,128)(2,1)} %param.15) | copy-start | bytes 1572868
  14.3 20.2 %copy-start.6 = (s32[1,1,128]{2,1,0:T(1,128)S(1)}, s32[1,1,128]{2,1,0:T(1,128)}, u32[]{:S(2)}) copy-start(s32[1,1,128]{2,1,0:T(1,128)} %param.17) | copy-start | bytes 1540
  14.3 20.9 %copy-start.7 = (s32[1,1,128]{2,1,0:T(1,128)S(1)}, s32[1,1,128]{2,1,0:T(1,128)}, u32[]{:S(2)}) copy-start(s32[1,1,128]{2,1,0:T(1,128)} %param.18) | copy-start | bytes 1540
  14.4 21.8 %copy-start.4 = (s32[1,1,32768]{2,1,0:T(1,128)S(1)}, s32[1,1,32768]{2,1,0:T(1,128)}, u32[]{:S(2)}) copy-start(s32[1,1,32768]{2,1,0:T(1,128)} %param.19) | copy-start | bytes 393220
  15.6 48.9 %all-to-all-start = ((bf16[128,8,512]{2,1,0:T(8,128)(2,1)}), bf16[128,8,512]{2,1,0:T(8,128)(2,1)S(1)}, u32[]{:S(2)}, u32[]{:S(2)}) async-start(bf16[128,8,512]{2,1,0:T(8,128)(2,1)} %bitcast_select_fusion), calls=%async_computation | async-start | bytes 2097152 | tf_op jit(solution)/shard_map/all_to_all | solution.py:40
  34.0 155.7 %all-reduce.6.cloned.1.call-start = ((), (), s32[]{:S(2)}) async-start(), calls=%async_computation.3 | async-start | bytes 4194304 | tf_op jit(solution)/shard_map/psum | solution.py:63
  46.1 18.3 %copy-start.2 = (bf16[1024,512]{1,0:T(8,128)(2,1)S(1)}, bf16[1024,512]{1,0:T(8,128)(2,1)}, u32[]{:S(2)}) copy-start(bf16[1024,512]{1,0:T(8,128)(2,1)} %param.13) | copy-start | bytes 3145732
  124.7 1.3 copy-start.1
  124.7 1.6 copy-start.5
  124.7 1.7 copy-start.3
  126.1 95.4 %all-gather.2.cloned.1.call-start = ((), (), s32[]{:S(2)}) async-start(), calls=%async_computation.4 | async-start | bytes 1310720 | tf_op jit(solution)/shard_map/all_gather | solution.py:82
  289.1 46.2 %all-to-all-start.1 = ((bf16[128,8,512]{2,1,0:T(8,128)(2,1)}), bf16[128,8,512]{2,1,0:T(8,128)(2,1)}, u32[]{:S(2)}, u32[]{:S(2)}) async-start(bf16[128,8,512]{2,1,0:T(8,128)(2,1)} %bitcast.21), calls=%async_computation.1 | async-start | bytes 2097152 | tf_op jit(solution)/shard_map/all_to_all | solution.py:101
  304.9 207.2 %all-reduce.8.cloned.1.call-start = ((), (), s32[]{:S(2)}) async-start(), calls=%async_computation.6 | async-start | bytes 4194304 | tf_op jit(solution)/shard_map/psum | solution.py:80
  309.7 249.3 %reduce-scatter.2.cloned.1.call-start = ((), (), s32[]{:S(2)}) async-start(), calls=%async_computation.5 | async-start | bytes 1310720 | tf_op jit(solution)/shard_map/reduce_scatter | solution.py:107
Sparse Core Ops, SparseCore 0:
  126.2 63.4 all-reduce.5
  193.2 28.2 all-gather.1
  309.9 202.1 all-reduce.7
  515.0 30.7 reduce-scatter.1
